TPU v7x, 256 devices: a whole 4x4x8 slice. The times are simulated.
256 devices in a mesh: tile: 32 (over z_hi, x, core), energy: 8 (over z_lo, y).
Axes of the slice: x: 4, y: 4, z: 8 (z_hi: 4, z_lo: 2; z = z_hi * 2 + z_lo), core: 2. Of those that a mesh axis runs over, the one named last changes fastest.
Arguments:
- object_tiles: float32 [8, 2, 8192, 256], P('energy', None, 'tile'), may hold values from -4 to 4
- probe_field: float32 [8, 2, 128, 128], P('energy'), may hold values from -4 to 4
- intensity: bfloat16 [8, 32, 8, 128, 128], P('energy', 'tile'), may hold values from 0.019897461 to 2
- row_offsets: int32 [32, 8], P('tile'), may hold values from -64 to 192, as said below
- col_offsets: int32 [32, 8], P('tile'), may hold values from 0 to 128
- tile_counts: int32 [32], P('tile'), may hold values from 3 to 8
- material_spectra: float32 [8, 3], replicated, may hold values from 0.2 to 2
Outputs:
- material_maps: float32 [3, 8192, 256], P(None, 'tile')
- model_object: float32 [8, 2, 8192, 256], P('energy', None, 'tile')
Inputs may be any that keep to these rules, and one draw needn't show every extreme that they name: `row_offsets`: in every tile one of slots 0 and 1 starts at -64 and the other at 192.
All inputs are finite; a program needn't handle non-finite values.
Results may differ from a plain program's by a relative error of at most 0.0003.
Values sent between devices are 32-bit elements; how exact they have to be, the bound alone decides.
A program may use at most 64 MiB of HBM per device.

v0:
```python
import math
import jax
import jax.numpy as jnp
from jax import lax
from jax.sharding import PartitionSpec as P

PROBE = 128
NN_ITERS = 8
SMOOTH = 0.01
DAMPING = 0.5


def with_halo(x, sides, width):
    for axis, dim in sides:
        count, length = (lax.axis_size(axis), x.shape[dim])
        up = [(i, (i + 1) % count) for i in range(count - 1)]
        down = [(j, i) for i, j in up]
        last = lax.slice_in_dim(x, length - width, length, axis=dim)
        initial = lax.slice_in_dim(x, 0, width, axis=dim)
        before = lax.ppermute(last, axis, up)
        after = lax.ppermute(initial, axis, down)
        x = jnp.concatenate([before, x, after], axis=dim)
    return x


def from_behind(value, axis, steps):
    count = lax.axis_size(axis)
    initial, last = (max(0, -steps), min(count, count - steps))
    return lax.ppermute(value, axis, [(source, source + steps) for source in range(initial, last)])


def left_apply(table, stack):
    return jnp.einsum(
        "jk,pkl->pjl",
        table,
        stack,
        precision=lax.Precision.HIGHEST,
        preferred_element_type=jnp.float32,
    )


def right_apply(stack, table):
    return jnp.einsum(
        "pjk,kl->pjl",
        stack,
        table,
        precision=lax.Precision.HIGHEST,
        preferred_element_type=jnp.float32,
    )


def tables(length):
    indices = jnp.arange(length, dtype=jnp.int32)
    angles = (
        2.0 * math.pi / length * (indices[:, None] * indices[None, :] % length).astype(jnp.float32)
    )
    return (jnp.cos(angles) / math.sqrt(length), jnp.sin(angles) / math.sqrt(length))


def transform(real_in, imag_in, cos_table, sin_table, direction):
    signed = direction * sin_table
    half_real = left_apply(cos_table, real_in) + left_apply(signed, imag_in)
    half_imag = left_apply(cos_table, imag_in) - left_apply(signed, real_in)
    out_real = right_apply(half_real, cos_table) + right_apply(half_imag, signed)
    out_imag = right_apply(half_imag, cos_table) - right_apply(half_real, signed)
    return (out_real, out_imag)


def unmix_maps(attenuation, spectra):
    step_size = 1.0 / jnp.sum(spectra * spectra)
    materials = jnp.zeros((spectra.shape[1],) + attenuation.shape[1:], attenuation.dtype)
    for iteration in range(NN_ITERS):
        predicted = jnp.sum(spectra[:, :, None, None] * materials[None], axis=1)
        mismatch = predicted - attenuation
        gradient = jnp.sum(spectra[:, :, None, None] * mismatch[:, None], axis=0)
        materials = jnp.maximum(materials - step_size * gradient, 0.0)
    return materials


def body(
    object_tiles, probe_field, intensity, row_offsets, col_offsets, tile_counts, material_spectra
):
    current = object_tiles[0]
    probe_re = probe_field[0, 0]
    probe_im = probe_field[0, 1]
    samples = intensity[0, 0]
    live_count = tile_counts[0]
    width = PROBE
    depth = PROBE // 2
    side = current.shape[1]
    slots = row_offsets.shape[1]
    cos_table, sin_table = tables(width)
    power = probe_re * probe_re + probe_im * probe_im
    row_starts = row_offsets[0] + depth
    col_starts = col_offsets[0]
    active = (jnp.arange(slots, dtype=jnp.int32) < live_count)[:, None, None]
    roots = jnp.sqrt(samples.astype(jnp.float32))
    extended = with_halo(current, (("tile", 1),), depth)

    def cut_window(row_start, col_start):
        anchor = jnp.zeros((), jnp.int32)
        return lax.dynamic_slice(extended, (anchor, row_start, col_start), (2, width, width))

    windows = jax.vmap(cut_window)(row_starts, col_starts)
    exit_re = probe_re * windows[:, 0] - probe_im * windows[:, 1]
    exit_im = probe_re * windows[:, 1] + probe_im * windows[:, 0]
    spec_re, spec_im = transform(exit_re, exit_im, cos_table, sin_table, 1.0)
    factor = roots / jnp.sqrt(spec_re * spec_re + spec_im * spec_im + SMOOTH)
    back_re, back_im = transform(spec_re * factor, spec_im * factor, cos_table, sin_table, -1.0)
    change_re = back_re - exit_re
    change_im = back_im - exit_im
    parts_re = jnp.where(active, probe_re * change_re + probe_im * change_im, 0.0)
    parts_im = jnp.where(active, probe_re * change_im - probe_im * change_re, 0.0)
    placed_power = jnp.where(active, power[None], 0.0)

    def place(position, totals):
        numerator, weights = totals
        row_start = row_starts[position]
        col_start = col_starts[position]
        anchor = jnp.zeros((), jnp.int32)
        parts = jnp.stack([parts_re[position], parts_im[position]])
        previous = lax.dynamic_slice(numerator, (anchor, row_start, col_start), (2, width, width))
        numerator = lax.dynamic_update_slice(
            numerator, previous + parts, (anchor, row_start, col_start)
        )
        older = lax.dynamic_slice(weights, (row_start, col_start), (width, width))
        weights = lax.dynamic_update_slice(
            weights, older + placed_power[position], (row_start, col_start)
        )
        return (numerator, weights)

    init = (jnp.zeros_like(extended), jnp.zeros_like(extended[0]))
    numerator, weights = lax.fori_loop(0, slots, place, init)
    from_above = from_behind((numerator[:, depth + side :], weights[depth + side :]), "tile", 1)
    from_below = from_behind((numerator[:, :depth], weights[:depth]), "tile", -1)
    core_num = numerator[:, depth : depth + side]
    core_weights = weights[depth : depth + side]
    core_num = core_num.at[:, :depth].add(from_above[0]).at[:, side - depth :].add(from_below[0])
    core_weights = core_weights.at[:depth].add(from_above[1]).at[side - depth :].add(from_below[1])
    current = current + core_num / (core_weights + DAMPING)
    squared = current[0] ** 2 + current[1] ** 2 + SMOOTH
    attenuation = -0.5 * jnp.log(squared)
    regrouped = lax.all_to_all(attenuation[None], "energy", split_axis=1, concat_axis=0, tiled=True)
    piece_maps = unmix_maps(regrouped, material_spectra)
    materials = lax.all_gather(piece_maps, "energy", axis=1, tiled=True)
    own_row = lax.dynamic_index_in_dim(
        material_spectra, lax.axis_index("energy"), 0, keepdims=False
    )
    thickness = jnp.sum(own_row[:, None, None] * materials, axis=0)
    scale_out = jnp.exp(-thickness) / jnp.sqrt(squared)
    model_object = (current * scale_out[None])[None]
    return (materials, model_object)


def solution(mesh):
    placed = (
        P("energy", None, "tile", None),
        P("energy", None, None, None),
        P("energy", "tile", None, None, None),
        P("tile", None),
        P("tile", None),
        P("tile"),
        P(),
    )
    return jax.shard_map(
        body,
        mesh=mesh,
        in_specs=placed,
        out_specs=(P(None, "tile", None), P("energy", None, "tile", None)),
        check_vma=False,
    )
```

profile of v0, /device:TPU:128, one launch (start us, length us, event | category | flops | bytes accessed | tf_op | source)
XLA Modules:
  0.0 357.7 jit_solution(117914211898438778)
XLA Ops:
  2.1 2.1 collective-permute-start
  4.2 7.9 %collective-permute-start.1 = (f32[2,64,256]{2,0,1:T(2,128)S(1)}, f32[2,64,256]{2,0,1:T(2,128)S(1)}, u32[]{:S(2)}, u32[]{:S(2)}) collective-permute-start(f32[2,64,256]{2,0,1:T(2,128)S(1)} %get-tuple-element.251), channel_id=1, source_target_pairs={{8,0},{16,8},{24,16},{32,24},{40,32},{48,40},{56,48},{64,56},{72,6... | collective-permute-start | bytes 393224 | tf_op jit(solution)/shard_map/ppermute | solution.py:21
  16.2 17.3 %while.21 = (s32[]{:T(128)}, f32[2,384,256]{2,0,1:T(2,128)S(1)}, s32[8,3]{0,1:T(4,128)S(1)}, f32[8,2,128,128]{3,2,0,1:T(8,128)S(1)}, s32[]{:T(128)}) while((s32[]{:T(128)}, f32[2,384,256]{2,0,1:T(2,128)S(1)}, s32[8,3]{0,1:T(4,128)S(1)}, f32[8,2,128,128]{3,2,0,1:T(8,128)S(1)}, s32[]{:T(128)}) %tuple.79), condition=%wide.while_cond.4, body=%wide.while_body.4.sunk | while | flops 2 | bytes 524405 | solution.py:102
  53.5 232.1 %while.20 = (s32[]{:T(128)}, f32[2,384,256]{2,0,1:T(2,128)S(1)}, f32[384,256]{1,0:T(8,128)S(1)}, s32[8]{0:T(128)S(1)}, s32[8]{0:T(128)S(1)}, /*index=5*/f32[8,12...) while((s32[]{:T(128)}, f32[2,384,256]{2,0,1:T(2,128)S(1)}, ...), condition=%wide.region_3.4_spmd, body=%wide.region_2.3_spmd.sunk | while | flops 81928 | bytes 1769713 | solution.py:133
  58.9 21.6 %dynamic_update_slice.16 = f32[2,384,256]{2,0,1:T(2,128)S(1)} dynamic-update-slice(f32[2,384,256]{2,0,1:T(2,128)S(1)} %get-tuple-element.369, f32[2,128,128]{2,0,1:T(2,128)S(1)} %copy.134, s32[]{:T(128)} %constant.183.clone.1..sunk, s32[]{:T(128)S(6)} %select_n.174, s32[]{:T(128)S(6)} %select_n.175) | dynamic-update-slice | bytes 262148 | tf_op jit(solution)/shard_map/while/body/eval_jaxpr/dynamic_update_slice | solution.py:123
  80.6 2.0 dynamic_update_slice.17
  88.1 21.6 %dynamic_update_slice.16 = f32[2,384,256]{2,0,1:T(2,128)S(1)} dynamic-update-slice(f32[2,384,256]{2,0,1:T(2,128)S(1)} %get-tuple-element.369, f32[2,128,128]{2,0,1:T(2,128)S(1)} %copy.134, s32[]{:T(128)} %constant.183.clone.1..sunk, s32[]{:T(128)S(6)} %select_n.174, s32[]{:T(128)S(6)} %select_n.175) | dynamic-update-slice | bytes 262148 | tf_op jit(solution)/shard_map/while/body/eval_jaxpr/dynamic_update_slice | solution.py:123
  116.8 21.6 %dynamic_update_slice.16 = f32[2,384,256]{2,0,1:T(2,128)S(1)} dynamic-update-slice(f32[2,384,256]{2,0,1:T(2,128)S(1)} %get-tuple-element.369, f32[2,128,128]{2,0,1:T(2,128)S(1)} %copy.134, s32[]{:T(128)} %constant.183.clone.1..sunk, s32[]{:T(128)S(6)} %select_n.174, s32[]{:T(128)S(6)} %select_n.175) | dynamic-update-slice | bytes 262148 | tf_op jit(solution)/shard_map/while/body/eval_jaxpr/dynamic_update_slice | solution.py:123
  145.7 21.6 %dynamic_update_slice.16 = f32[2,384,256]{2,0,1:T(2,128)S(1)} dynamic-update-slice(f32[2,384,256]{2,0,1:T(2,128)S(1)} %get-tuple-element.369, f32[2,128,128]{2,0,1:T(2,128)S(1)} %copy.134, s32[]{:T(128)} %constant.183.clone.1..sunk, s32[]{:T(128)S(6)} %select_n.174, s32[]{:T(128)S(6)} %select_n.175) | dynamic-update-slice | bytes 262148 | tf_op jit(solution)/shard_map/while/body/eval_jaxpr/dynamic_update_slice | solution.py:123
  167.4 2.0 dynamic_update_slice.17
  174.9 21.6 %dynamic_update_slice.16 = f32[2,384,256]{2,0,1:T(2,128)S(1)} dynamic-update-slice(f32[2,384,256]{2,0,1:T(2,128)S(1)} %get-tuple-element.369, f32[2,128,128]{2,0,1:T(2,128)S(1)} %copy.134, s32[]{:T(128)} %constant.183.clone.1..sunk, s32[]{:T(128)S(6)} %select_n.174, s32[]{:T(128)S(6)} %select_n.175) | dynamic-update-slice | bytes 262148 | tf_op jit(solution)/shard_map/while/body/eval_jaxpr/dynamic_update_slice | solution.py:123
  203.8 21.6 %dynamic_update_slice.16 = f32[2,384,256]{2,0,1:T(2,128)S(1)} dynamic-update-slice(f32[2,384,256]{2,0,1:T(2,128)S(1)} %get-tuple-element.369, f32[2,128,128]{2,0,1:T(2,128)S(1)} %copy.134, s32[]{:T(128)} %constant.183.clone.1..sunk, s32[]{:T(128)S(6)} %select_n.174, s32[]{:T(128)S(6)} %select_n.175) | dynamic-update-slice | bytes 262148 | tf_op jit(solution)/shard_map/while/body/eval_jaxpr/dynamic_update_slice | solution.py:123
  225.4 1.9 dynamic_update_slice.17
  232.8 21.6 %dynamic_update_slice.16 = f32[2,384,256]{2,0,1:T(2,128)S(1)} dynamic-update-slice(f32[2,384,256]{2,0,1:T(2,128)S(1)} %get-tuple-element.369, f32[2,128,128]{2,0,1:T(2,128)S(1)} %copy.134, s32[]{:T(128)} %constant.183.clone.1..sunk, s32[]{:T(128)S(6)} %select_n.174, s32[]{:T(128)S(6)} %select_n.175) | dynamic-update-slice | bytes 262148 | tf_op jit(solution)/shard_map/while/body/eval_jaxpr/dynamic_update_slice | solution.py:123
  254.5 2.0 dynamic_update_slice.17
  262.0 21.6 %dynamic_update_slice.16 = f32[2,384,256]{2,0,1:T(2,128)S(1)} dynamic-update-slice(f32[2,384,256]{2,0,1:T(2,128)S(1)} %get-tuple-element.369, f32[2,128,128]{2,0,1:T(2,128)S(1)} %copy.134, s32[]{:T(128)} %constant.183.clone.1..sunk, s32[]{:T(128)S(6)} %select_n.174, s32[]{:T(128)S(6)} %select_n.175) | dynamic-update-slice | bytes 262148 | tf_op jit(solution)/shard_map/while/body/eval_jaxpr/dynamic_update_slice | solution.py:123
  285.6 1.9 collective-permute-start.4
  287.7 7.9 %collective-permute-start.5 = (f32[64,256]{1,0:T(8,128)S(1)}, f32[64,256]{1,0:T(8,128)S(1)}, u32[]{:S(2)}, u32[]{:S(2)}) collective-permute-start(f32[64,256]{1,0:T(8,128)S(1)} %get-tuple-element.252), channel_id=1, source_target_pairs={{8,0},{16,8},{24,16},{32,24},{40,32},{48,40},{56,48},{64,56},{72,6... | collective-permute-start | bytes 196616 | tf_op jit(solution)/shard_map/ppermute | solution.py:29
  295.6 1.9 collective-permute-start.2
  297.5 8.1 %collective-permute-start.3 = (f32[2,64,256]{2,0,1:T(2,128)S(1)}, f32[2,64,256]{2,0,1:T(2,128)S(1)}, u32[]{:S(2)}, u32[]{:S(2)}) collective-permute-start(f32[2,64,256]{2,0,1:T(2,128)S(1)} %get-tuple-element.248), channel_id=1, source_target_pairs={{8,0},{16,8},{24,16},{32,24},{40,32},{48,40},{56,48},{64,56},{72,6... | collective-permute-start | bytes 393224 | tf_op jit(solution)/shard_map/ppermute | solution.py:29
  306.2 3.0 collective-permute-done.3
  311.3 4.5 %all-to-all-start = ((f32[1,256,256]{2,0,1:T(1,128)}), f32[1,256,256]{2,0,1:T(1,128)S(1)}, u32[]{:S(2)}, u32[]{:S(2)}) async-start(f32[1,256,256]{2,0,1:T(1,128)} %get-tuple-element.238), calls=%async_computation | async-start | bytes 524288 | tf_op jit(solution)/shard_map/all_to_all | solution.py:143
  317.3 5.7 %all-to-all-done = f32[1,256,256]{2,0,1:T(1,128)S(1)} async-done(((f32[1,256,256]{2,0,1:T(1,128)}), f32[1,256,256]{2,0,1:T(1,128)S(1)}, u32[]{:S(2)}, u32[]{:S(2)}) %all-to-all-start) | async-done | bytes 262176 | tf_op jit(solution)/shard_map/all_to_all | solution.py:143
  325.5 29.7 %all_gather.3 = f32[3,256,256]{2,1,0:T(8,128)S(1)} all-gather(f32[3,32,256]{2,1,0:T(8,128)S(1)} %subtract_maximum_fusion), channel_id=1, replica_groups=mesh['tile'=32,'energy'=8] {'energy'}, dimensions={1}, use_global_device_ids=true | all-gather | bytes 884736 | tf_op jit(solution)/shard_map/all_gather | solution.py:145
  (192 shorter events, 70.0 us)
Async XLA Ops:
  2.1 10.0 %copy-start.2 = (f32[1,2,128,128]{3,2,1,0:T(8,128)S(1)}, f32[1,2,128,128]{3,2,1,0:T(8,128)}, u32[]{:S(2)}) copy-start(f32[1,2,128,128]{3,2,1,0:T(8,128)} %param.18) | copy-start | bytes 393220
  2.1 12.0 %collective-permute-start = (f32[2,64,256]{2,0,1:T(2,128)S(1)}, f32[2,64,256]{2,0,1:T(2,128)S(1)}, u32[]{:S(2)}, u32[]{:S(2)}) collective-permute-start(f32[2,64,256]{2,0,1:T(2,128)S(1)} %get-tuple-element.250), channel_id=1, source_target_pairs={{0,8},{8,16},{16,24},{24,32},{32,40},{40,48},{48,56},{56,64},{64,7... | collective-permute-start | bytes 393224 | tf_op jit(solution)/shard_map/ppermute | solution.py:20
  4.2 11.6 %collective-permute-start.1 = (f32[2,64,256]{2,0,1:T(2,128)S(1)}, f32[2,64,256]{2,0,1:T(2,128)S(1)}, u32[]{:S(2)}, u32[]{:S(2)}) collective-permute-start(f32[2,64,256]{2,0,1:T(2,128)S(1)} %get-tuple-element.251), channel_id=1, source_target_pairs={{8,0},{16,8},{24,16},{32,24},{40,32},{48,40},{56,48},{64,56},{72,6... | collective-permute-start | bytes 393224 | tf_op jit(solution)/shard_map/ppermute | solution.py:21
  12.1 0.7 copy-start.4
  12.7 0.7 copy-start.5
  41.6 1.2 copy-start
  285.6 20.1 %collective-permute-start.4 = (f32[64,256]{1,0:T(8,128)S(1)}, f32[64,256]{1,0:T(8,128)S(1)}, u32[]{:S(2)}, u32[]{:S(2)}) collective-permute-start(f32[64,256]{1,0:T(8,128)S(1)} %get-tuple-element.253), channel_id=1, source_target_pairs={{0,8},{8,16},{16,24},{24,32},{32,40},{40,48},{48,56},{56,64},{64,7... | collective-permute-start | bytes 196616 | tf_op jit(solution)/shard_map/ppermute | solution.py:29
  287.7 17.9 %collective-permute-start.5 = (f32[64,256]{1,0:T(8,128)S(1)}, f32[64,256]{1,0:T(8,128)S(1)}, u32[]{:S(2)}, u32[]{:S(2)}) collective-permute-start(f32[64,256]{1,0:T(8,128)S(1)} %get-tuple-element.252), channel_id=1, source_target_pairs={{8,0},{16,8},{24,16},{32,24},{40,32},{48,40},{56,48},{64,56},{72,6... | collective-permute-start | bytes 196616 | tf_op jit(solution)/shard_map/ppermute | solution.py:29
  295.6 10.5 %collective-permute-start.2 = (f32[2,64,256]{2,0,1:T(2,128)S(1)}, f32[2,64,256]{2,0,1:T(2,128)S(1)}, u32[]{:S(2)}, u32[]{:S(2)}) collective-permute-start(f32[2,64,256]{2,0,1:T(2,128)S(1)} %get-tuple-element.249), channel_id=1, source_target_pairs={{0,8},{8,16},{16,24},{24,32},{32,40},{40,48},{48,56},{56,64},{64,7... | collective-permute-start | bytes 393224 | tf_op jit(solution)/shard_map/ppermute | solution.py:29
  297.5 11.7 %collective-permute-start.3 = (f32[2,64,256]{2,0,1:T(2,128)S(1)}, f32[2,64,256]{2,0,1:T(2,128)S(1)}, u32[]{:S(2)}, u32[]{:S(2)}) collective-permute-start(f32[2,64,256]{2,0,1:T(2,128)S(1)} %get-tuple-element.248), channel_id=1, source_target_pairs={{8,0},{16,8},{24,16},{32,24},{40,32},{48,40},{56,48},{64,56},{72,6... | collective-permute-start | bytes 393224 | tf_op jit(solution)/shard_map/ppermute | solution.py:29
  305.7 3.6 %copy-start.1 = (f32[1,2,256,256]{3,2,1,0:T(8,128)S(1)}, f32[1,2,256,256]{3,2,1,0:T(8,128)}, u32[]{:S(2)}) copy-start(f32[1,2,256,256]{3,2,1,0:T(8,128)} %param.17) | copy-start | bytes 1572868
  309.9 5.8 %copy-start.3 = (f32[8,3]{0,1:T(4,128)S(1)}, f32[8,3]{0,1:T(4,128)}, u32[]{:S(2)}) copy-start(f32[8,3]{0,1:T(4,128)} %param.23) | copy-start | bytes 292
  311.3 11.7 %all-to-all-start = ((f32[1,256,256]{2,0,1:T(1,128)}), f32[1,256,256]{2,0,1:T(1,128)S(1)}, u32[]{:S(2)}, u32[]{:S(2)}) async-start(f32[1,256,256]{2,0,1:T(1,128)} %get-tuple-element.238), calls=%async_computation | async-start | bytes 524288 | tf_op jit(solution)/shard_map/all_to_all | solution.py:143
where the time goes:
time: 359 us; the launch traced here: 358 us
  local copies, waits for them, and re-layouts  222 us (62%)
  starting transfers between devices  34.2 us (10%)
  loops' own time  31.8 us (9%)
  blocking collectives  29.7 us (8%)
  matrix products  19.5 us (5%)
  waiting for transfers between devices  10.8 us (3%)
  other arithmetic  7.17 us (2%)
    dynamic_update_slice x16, local copies, waits for them, and re-layouts, place(): lax.dynamic_update_slice(numerator, previous + parts, (anchor, row_start,...  173 us
    another operation x1, loops' own time, body(): numerator, weights = lax.fori_loop(0, slots, place, init)  31.6 us
    all_gather x1, blocking collectives, body(): materials = lax.all_gather(piece_maps, 'energy', axis=1, tiled=True)  29.7 us
    ppermute x4, starting transfers between devices, from_behind(): lax.ppermute(value, axis, [(source, source + steps) for source in range(i...  19.8 us
    gather x32, local copies, waits for them, and re-layouts  17.1 us
    dynamic_update_slice x8, local copies, waits for them, and re-layouts, place(): lax.dynamic_update_slice(weights, older + placed_power[position], (row_st...  14.9 us
    dot_general x8, matrix products, left_apply(): jnp.einsum('jk,pkl->pjl', table, stack, precision=lax.Precision.HIGHEST,...  10.3 us
    dot_general x8, matrix products, right_apply(): jnp.einsum('pjk,kl->pjl', stack, table, precision=lax.Precision.HIGHEST,...  9.19 us
  transfers between devices with their start and end apart: 7, of which 4 were waited for; matrix products, arithmetic and copies ran while one was open for 0% of the time, Pallas kernels for 0%

commit v1 on v0

--- a/solution.py
+++ b/solution.py
@@ -142,7 +142,9 @@
     attenuation = -0.5 * jnp.log(squared)
     regrouped = lax.all_to_all(attenuation[None], "energy", split_axis=1, concat_axis=0, tiled=True)
     piece_maps = unmix_maps(regrouped, material_spectra)
-    materials = lax.all_gather(piece_maps, "energy", axis=1, tiled=True)
+    materials = jnp.concatenate(
+        lax.all_to_all(jnp.stack([piece_maps] * lax.axis_size("energy")), "energy", 0, 0), axis=1
+    )
     own_row = lax.dynamic_index_in_dim(
         material_spectra, lax.axis_index("energy"), 0, keepdims=False
     )

time: 359 us -> 345 us (0.961)
  blocking collectives: 29.7 us -> 0 us
  waiting for transfers between devices: 10.8 us -> 20.2 us
  starting transfers between devices: 34.2 us -> 37.8 us
    all_gather x1 -> x0, blocking collectives: 29.7 us -> none  [body(): materials = lax.all_gather(piece_maps, 'energy', axis=1, tiled=True)]
    all_to_all x0 -> x1, waiting for transfers between devices: none -> 9.22 us  [body(): lax.all_to_all(jnp.stack([piece_maps] * lax.axis_size('energy')), 'energy...]
  transfers between devices with their start and end apart: 7 -> 8, of which waited for: 4 -> 5; matrix products, arithmetic and copies ran while one was open for 0% -> 0% of each run, Pallas kernels for 0% -> 0%
where the time goes in v1:
time: 345 us; the launch traced here: 342 us
  local copies, waits for them, and re-layouts  223 us (65%)
  starting transfers between devices  37.8 us (11%)
  loops' own time  31.8 us (9%)
  waiting for transfers between devices  20.2 us (6%)
  matrix products  19.5 us (6%)
  other arithmetic  6.93 us (2%)
    dynamic_update_slice x16, local copies, waits for them, and re-layouts, place(): lax.dynamic_update_slice(numerator, previous + parts, (anchor, row_start,...  173 us
    another operation x1, loops' own time, body(): numerator, weights = lax.fori_loop(0, slots, place, init)  31.6 us
    ppermute x4, starting transfers between devices, from_behind(): lax.ppermute(value, axis, [(source, source + steps) for source in range(i...  19.8 us
    gather x32, local copies, waits for them, and re-layouts  17.1 us
    dynamic_update_slice x8, local copies, waits for them, and re-layouts, place(): lax.dynamic_update_slice(weights, older + placed_power[position], (row_st...  14.9 us
    dot_general x8, matrix products, left_apply(): jnp.einsum('jk,pkl->pjl', table, stack, precision=lax.Precision.HIGHEST,...  10.3 us
    all_to_all x1, waiting for transfers between devices, body(): lax.all_to_all(jnp.stack([piece_maps] * lax.axis_size('energy')), 'energy...  9.22 us
    dot_general x8, matrix products, right_apply(): jnp.einsum('pjk,kl->pjl', stack, table, precision=lax.Precision.HIGHEST,...  9.19 us
  transfers between devices with their start and end apart: 8, of which 5 were waited for; matrix products, arithmetic and copies ran while one was open for 0% of the time, Pallas kernels for 0%

profile of v1, /device:TPU:128, one launch (start us, length us, event | category | flops | bytes accessed | tf_op | source)
XLA Modules:
  0.0 342.1 jit_solution(1986755218629877186)
XLA Ops:
  2.1 2.1 collective-permute-start
  4.2 7.9 %collective-permute-start.1 = (f32[2,64,256]{2,0,1:T(2,128)S(1)}, f32[2,64,256]{2,0,1:T(2,128)S(1)}, u32[]{:S(2)}, u32[]{:S(2)}) collective-permute-start(f32[2,64,256]{2,0,1:T(2,128)S(1)} %get-tuple-element.257), channel_id=1, source_target_pairs={{8,0},{16,8},{24,16},{32,24},{40,32},{48,40},{56,48},{64,56},{72,6... | collective-permute-start | bytes 393224 | tf_op jit(solution)/shard_map/ppermute | solution.py:21
  16.2 17.3 %while.21 = (s32[]{:T(128)}, f32[2,384,256]{2,0,1:T(2,128)S(1)}, s32[8,3]{0,1:T(4,128)S(1)}, f32[8,2,128,128]{3,2,0,1:T(8,128)S(1)}, s32[]{:T(128)}) while((s32[]{:T(128)}, f32[2,384,256]{2,0,1:T(2,128)S(1)}, s32[8,3]{0,1:T(4,128)S(1)}, f32[8,2,128,128]{3,2,0,1:T(8,128)S(1)}, s32[]{:T(128)}) %tuple.81), condition=%wide.while_cond.4, body=%wide.while_body.4.sunk | while | flops 2 | bytes 524405 | solution.py:102
  53.5 232.1 %while.20 = (s32[]{:T(128)}, f32[2,384,256]{2,0,1:T(2,128)S(1)}, f32[384,256]{1,0:T(8,128)S(1)}, s32[8]{0:T(128)S(1)}, s32[8]{0:T(128)S(1)}, /*index=5*/f32[8,12...) while((s32[]{:T(128)}, f32[2,384,256]{2,0,1:T(2,128)S(1)}, ...), condition=%wide.region_3.4_spmd, body=%wide.region_2.3_spmd.sunk | while | flops 81928 | bytes 1769713 | solution.py:133
  58.9 21.6 %dynamic_update_slice.16 = f32[2,384,256]{2,0,1:T(2,128)S(1)} dynamic-update-slice(f32[2,384,256]{2,0,1:T(2,128)S(1)} %get-tuple-element.375, f32[2,128,128]{2,0,1:T(2,128)S(1)} %copy.163, s32[]{:T(128)} %constant.183.clone.1..sunk, s32[]{:T(128)S(6)} %select_n.174, s32[]{:T(128)S(6)} %select_n.175) | dynamic-update-slice | bytes 262148 | tf_op jit(solution)/shard_map/while/body/eval_jaxpr/dynamic_update_slice | solution.py:123
  80.6 2.0 dynamic_update_slice.17
  88.1 21.6 %dynamic_update_slice.16 = f32[2,384,256]{2,0,1:T(2,128)S(1)} dynamic-update-slice(f32[2,384,256]{2,0,1:T(2,128)S(1)} %get-tuple-element.375, f32[2,128,128]{2,0,1:T(2,128)S(1)} %copy.163, s32[]{:T(128)} %constant.183.clone.1..sunk, s32[]{:T(128)S(6)} %select_n.174, s32[]{:T(128)S(6)} %select_n.175) | dynamic-update-slice | bytes 262148 | tf_op jit(solution)/shard_map/while/body/eval_jaxpr/dynamic_update_slice | solution.py:123
  116.8 21.6 %dynamic_update_slice.16 = f32[2,384,256]{2,0,1:T(2,128)S(1)} dynamic-update-slice(f32[2,384,256]{2,0,1:T(2,128)S(1)} %get-tuple-element.375, f32[2,128,128]{2,0,1:T(2,128)S(1)} %copy.163, s32[]{:T(128)} %constant.183.clone.1..sunk, s32[]{:T(128)S(6)} %select_n.174, s32[]{:T(128)S(6)} %select_n.175) | dynamic-update-slice | bytes 262148 | tf_op jit(solution)/shard_map/while/body/eval_jaxpr/dynamic_update_slice | solution.py:123
  145.7 21.6 %dynamic_update_slice.16 = f32[2,384,256]{2,0,1:T(2,128)S(1)} dynamic-update-slice(f32[2,384,256]{2,0,1:T(2,128)S(1)} %get-tuple-element.375, f32[2,128,128]{2,0,1:T(2,128)S(1)} %copy.163, s32[]{:T(128)} %constant.183.clone.1..sunk, s32[]{:T(128)S(6)} %select_n.174, s32[]{:T(128)S(6)} %select_n.175) | dynamic-update-slice | bytes 262148 | tf_op jit(solution)/shard_map/while/body/eval_jaxpr/dynamic_update_slice | solution.py:123
  167.4 2.0 dynamic_update_slice.17
  174.9 21.6 %dynamic_update_slice.16 = f32[2,384,256]{2,0,1:T(2,128)S(1)} dynamic-update-slice(f32[2,384,256]{2,0,1:T(2,128)S(1)} %get-tuple-element.375, f32[2,128,128]{2,0,1:T(2,128)S(1)} %copy.163, s32[]{:T(128)} %constant.183.clone.1..sunk, s32[]{:T(128)S(6)} %select_n.174, s32[]{:T(128)S(6)} %select_n.175) | dynamic-update-slice | bytes 262148 | tf_op jit(solution)/shard_map/while/body/eval_jaxpr/dynamic_update_slice | solution.py:123
  203.8 21.6 %dynamic_update_slice.16 = f32[2,384,256]{2,0,1:T(2,128)S(1)} dynamic-update-slice(f32[2,384,256]{2,0,1:T(2,128)S(1)} %get-tuple-element.375, f32[2,128,128]{2,0,1:T(2,128)S(1)} %copy.163, s32[]{:T(128)} %constant.183.clone.1..sunk, s32[]{:T(128)S(6)} %select_n.174, s32[]{:T(128)S(6)} %select_n.175) | dynamic-update-slice | bytes 262148 | tf_op jit(solution)/shard_map/while/body/eval_jaxpr/dynamic_update_slice | solution.py:123
  232.8 21.6 %dynamic_update_slice.16 = f32[2,384,256]{2,0,1:T(2,128)S(1)} dynamic-update-slice(f32[2,384,256]{2,0,1:T(2,128)S(1)} %get-tuple-element.375, f32[2,128,128]{2,0,1:T(2,128)S(1)} %copy.163, s32[]{:T(128)} %constant.183.clone.1..sunk, s32[]{:T(128)S(6)} %select_n.174, s32[]{:T(128)S(6)} %select_n.175) | dynamic-update-slice | bytes 262148 | tf_op jit(solution)/shard_map/while/body/eval_jaxpr/dynamic_update_slice | solution.py:123
  254.5 2.0 dynamic_update_slice.17
  262.0 21.6 %dynamic_update_slice.16 = f32[2,384,256]{2,0,1:T(2,128)S(1)} dynamic-update-slice(f32[2,384,256]{2,0,1:T(2,128)S(1)} %get-tuple-element.375, f32[2,128,128]{2,0,1:T(2,128)S(1)} %copy.163, s32[]{:T(128)} %constant.183.clone.1..sunk, s32[]{:T(128)S(6)} %select_n.174, s32[]{:T(128)S(6)} %select_n.175) | dynamic-update-slice | bytes 262148 | tf_op jit(solution)/shard_map/while/body/eval_jaxpr/dynamic_update_slice | solution.py:123
  285.6 1.9 collective-permute-start.4
  287.7 7.9 %collective-permute-start.5 = (f32[64,256]{1,0:T(8,128)S(1)}, f32[64,256]{1,0:T(8,128)S(1)}, u32[]{:S(2)}, u32[]{:S(2)}) collective-permute-start(f32[64,256]{1,0:T(8,128)S(1)} %get-tuple-element.258), channel_id=1, source_target_pairs={{8,0},{16,8},{24,16},{32,24},{40,32},{48,40},{56,48},{64,56},{72,6... | collective-permute-start | bytes 196616 | tf_op jit(solution)/shard_map/ppermute | solution.py:29
  295.6 1.9 collective-permute-start.2
  297.5 8.1 %collective-permute-start.3 = (f32[2,64,256]{2,0,1:T(2,128)S(1)}, f32[2,64,256]{2,0,1:T(2,128)S(1)}, u32[]{:S(2)}, u32[]{:S(2)}) collective-permute-start(f32[2,64,256]{2,0,1:T(2,128)S(1)} %get-tuple-element.254), channel_id=1, source_target_pairs={{8,0},{16,8},{24,16},{32,24},{40,32},{48,40},{56,48},{64,56},{72,6... | collective-permute-start | bytes 393224 | tf_op jit(solution)/shard_map/ppermute | solution.py:29
  306.2 3.0 collective-permute-done.3
  311.3 4.6 %all-to-all-start = ((f32[1,256,256]{2,0,1:T(1,128)}), f32[1,256,256]{2,0,1:T(1,128)S(1)}, u32[]{:S(2)}, u32[]{:S(2)}) async-start(f32[1,256,256]{2,0,1:T(1,128)} %get-tuple-element.244), calls=%async_computation | async-start | bytes 524288 | tf_op jit(solution)/shard_map/all_to_all | solution.py:143
  317.3 5.8 %all-to-all-done = f32[1,256,256]{2,0,1:T(1,128)S(1)} async-done(((f32[1,256,256]{2,0,1:T(1,128)}), f32[1,256,256]{2,0,1:T(1,128)S(1)}, u32[]{:S(2)}, u32[]{:S(2)}) %all-to-all-start) | async-done | bytes 262176 | tf_op jit(solution)/shard_map/all_to_all | solution.py:143
  326.6 3.5 %all-to-all-start.1 = ((f32[8,3,32,256]{3,2,1,0:T(8,128)}), f32[8,3,32,256]{3,2,1,0:T(8,128)S(1)}, u32[]{:S(2)}, u32[]{:S(2)}) async-start(f32[8,3,32,256]{3,2,1,0:T(8,128)} %stack.9), calls=%async_computation.1 | async-start | bytes 1572864 | tf_op jit(solution)/shard_map/all_to_all | solution.py:146
  330.3 9.2 %all-to-all-done.1 = f32[8,3,32,256]{3,2,1,0:T(8,128)S(1)} async-done(((f32[8,3,32,256]{3,2,1,0:T(8,128)}), f32[8,3,32,256]{3,2,1,0:T(8,128)S(1)}, u32[]{:S(2)}, u32[]{:S(2)}) %all-to-all-start.1) | async-done | bytes 786464 | tf_op jit(solution)/shard_map/all_to_all | solution.py:146
  (195 shorter events, 73.0 us)
Async XLA Ops:
  2.1 10.0 %copy-start.2 = (f32[1,2,128,128]{3,2,1,0:T(8,128)S(1)}, f32[1,2,128,128]{3,2,1,0:T(8,128)}, u32[]{:S(2)}) copy-start(f32[1,2,128,128]{3,2,1,0:T(8,128)} %param.18) | copy-start | bytes 393220
  2.1 12.0 %collective-permute-start = (f32[2,64,256]{2,0,1:T(2,128)S(1)}, f32[2,64,256]{2,0,1:T(2,128)S(1)}, u32[]{:S(2)}, u32[]{:S(2)}) collective-permute-start(f32[2,64,256]{2,0,1:T(2,128)S(1)} %get-tuple-element.256), channel_id=1, source_target_pairs={{0,8},{8,16},{16,24},{24,32},{32,40},{40,48},{48,56},{56,64},{64,7... | collective-permute-start | bytes 393224 | tf_op jit(solution)/shard_map/ppermute | solution.py:20
  4.2 11.6 %collective-permute-start.1 = (f32[2,64,256]{2,0,1:T(2,128)S(1)}, f32[2,64,256]{2,0,1:T(2,128)S(1)}, u32[]{:S(2)}, u32[]{:S(2)}) collective-permute-start(f32[2,64,256]{2,0,1:T(2,128)S(1)} %get-tuple-element.257), channel_id=1, source_target_pairs={{8,0},{16,8},{24,16},{32,24},{40,32},{48,40},{56,48},{64,56},{72,6... | collective-permute-start | bytes 393224 | tf_op jit(solution)/shard_map/ppermute | solution.py:21
  12.1 0.7 copy-start.4
  12.7 0.7 copy-start.5
  41.6 1.2 copy-start
  285.6 20.1 %collective-permute-start.4 = (f32[64,256]{1,0:T(8,128)S(1)}, f32[64,256]{1,0:T(8,128)S(1)}, u32[]{:S(2)}, u32[]{:S(2)}) collective-permute-start(f32[64,256]{1,0:T(8,128)S(1)} %get-tuple-element.259), channel_id=1, source_target_pairs={{0,8},{8,16},{16,24},{24,32},{32,40},{40,48},{48,56},{56,64},{64,7... | collective-permute-start | bytes 196616 | tf_op jit(solution)/shard_map/ppermute | solution.py:29
  287.7 17.9 %collective-permute-start.5 = (f32[64,256]{1,0:T(8,128)S(1)}, f32[64,256]{1,0:T(8,128)S(1)}, u32[]{:S(2)}, u32[]{:S(2)}) collective-permute-start(f32[64,256]{1,0:T(8,128)S(1)} %get-tuple-element.258), channel_id=1, source_target_pairs={{8,0},{16,8},{24,16},{32,24},{40,32},{48,40},{56,48},{64,56},{72,6... | collective-permute-start | bytes 196616 | tf_op jit(solution)/shard_map/ppermute | solution.py:29
  295.6 10.5 %collective-permute-start.2 = (f32[2,64,256]{2,0,1:T(2,128)S(1)}, f32[2,64,256]{2,0,1:T(2,128)S(1)}, u32[]{:S(2)}, u32[]{:S(2)}) collective-permute-start(f32[2,64,256]{2,0,1:T(2,128)S(1)} %get-tuple-element.255), channel_id=1, source_target_pairs={{0,8},{8,16},{16,24},{24,32},{32,40},{40,48},{48,56},{56,64},{64,7... | collective-permute-start | bytes 393224 | tf_op jit(solution)/shard_map/ppermute | solution.py:29
  297.5 11.7 %collective-permute-start.3 = (f32[2,64,256]{2,0,1:T(2,128)S(1)}, f32[2,64,256]{2,0,1:T(2,128)S(1)}, u32[]{:S(2)}, u32[]{:S(2)}) collective-permute-start(f32[2,64,256]{2,0,1:T(2,128)S(1)} %get-tuple-element.254), channel_id=1, source_target_pairs={{8,0},{16,8},{24,16},{32,24},{40,32},{48,40},{56,48},{64,56},{72,6... | collective-permute-start | bytes 393224 | tf_op jit(solution)/shard_map/ppermute | solution.py:29
  305.7 3.6 %copy-start.1 = (f32[1,2,256,256]{3,2,1,0:T(8,128)S(1)}, f32[1,2,256,256]{3,2,1,0:T(8,128)}, u32[]{:S(2)}) copy-start(f32[1,2,256,256]{3,2,1,0:T(8,128)} %param.17) | copy-start | bytes 1572868
  311.3 4.6 %copy-start.3 = (f32[8,3]{0,1:T(4,128)S(1)}, f32[8,3]{0,1:T(4,128)}, u32[]{:S(2)}) copy-start(f32[8,3]{0,1:T(4,128)} %param.23) | copy-start | bytes 292
  311.3 11.8 %all-to-all-start = ((f32[1,256,256]{2,0,1:T(1,128)}), f32[1,256,256]{2,0,1:T(1,128)S(1)}, u32[]{:S(2)}, u32[]{:S(2)}) async-start(f32[1,256,256]{2,0,1:T(1,128)} %get-tuple-element.244), calls=%async_computation | async-start | bytes 524288 | tf_op jit(solution)/shard_map/all_to_all | solution.py:143
  326.6 13.0 %all-to-all-start.1 = ((f32[8,3,32,256]{3,2,1,0:T(8,128)}), f32[8,3,32,256]{3,2,1,0:T(8,128)S(1)}, u32[]{:S(2)}, u32[]{:S(2)}) async-start(f32[8,3,32,256]{3,2,1,0:T(8,128)} %stack.9), calls=%async_computation.1 | async-start | bytes 1572864 | tf_op jit(solution)/shard_map/all_to_all | solution.py:146
